TPU v7x, 32 devices: a whole 2x2x4 slice. The times are simulated.
32 devices in a mesh: blk: 4 (over x, core), uly: 8 (over z, y).
Axes of the slice: x: 2, y: 2, z: 4, core: 2. Of those that a mesh axis runs over, the one named last changes fastest.
Arguments:
- query_rows: bfloat16 [4096, 512], P(('blk', 'uly')), may hold values from -6 to 6
- key_rows: bfloat16 [4096, 512], P(('blk', 'uly')), may hold values from -6 to 6
- value_rows: bfloat16 [4096, 512], P(('blk', 'uly')), may hold values from -6 to 6
- out_grad: bfloat16 [4096, 512], P(('blk', 'uly')), may hold values from -6 to 6
- block_lists: int32 [64, 8], P('blk'), may hold values from 0 to 63, as said below
- block_counts: int32 [64], P('blk'), may hold values from 1 to 8
Outputs:
- attended: bfloat16 [4096, 512], P(('blk', 'uly'))
- query_gradient: bfloat16 [4096, 512], P(('blk', 'uly'))
- key_grad: bfloat16 [4096, 512], P(('blk', 'uly'))
- value_grad: bfloat16 [4096, 512], P(('blk', 'uly'))
Inputs may be any that keep to these rules, and one draw needn't show every extreme that they name: `block_lists`: row b lists key blocks of query block b: entry 0 is b, entries 1 to block_counts[b] - 1 are distinct blocks other than b, and the remaining entries equal b.
All inputs are finite; a program needn't handle non-finite values.
Results may differ from a plain program's by a relative error of at most 0.02.
Values may be sent and summed in bfloat16 or wider, within the bound.
A program may use at most 128 MiB of HBM per device.

v0:
```python
import math
import jax
import jax.numpy as jnp
from jax import lax
from jax.sharding import PartitionSpec as P

HDIM = 64
BLK = 64
KSEL = 8


def fetch_sets(pair_blocks, list_group, count_group):
    picked = pair_blocks[list_group]
    usable = (jnp.arange(KSEL)[None, :] < count_group[:, None])[:, None, None, :, None]
    return (picked[..., :HDIM], picked[..., HDIM:], usable)


def probabilities(query_group, gathered_key_blocks, usable):
    logit_matrix = jnp.einsum(
        "gqhd,gjkhd->gqhjk", query_group, gathered_key_blocks, preferred_element_type=jnp.float32
    ) * (1.0 / math.sqrt(HDIM))
    row_max = jnp.max(jnp.where(usable, logit_matrix, -1e30), axis=(3, 4), keepdims=True)
    weights = jnp.where(usable, jnp.exp(logit_matrix - row_max), 0.0)
    return weights / jnp.sum(weights, axis=(3, 4), keepdims=True)


def attend(reduced_precision, gathered_value_blocks):
    return jnp.einsum(
        "gqhjk,gjkhd->gqhd",
        reduced_precision,
        gathered_value_blocks,
        preferred_element_type=jnp.float32,
    ).astype(jnp.bfloat16)


def backward_group(
    gathered_key_blocks,
    gathered_value_blocks,
    query_group,
    grad_group,
    out_group,
    probability,
    reduced_precision,
):
    softmax_scale = 1.0 / math.sqrt(HDIM)
    delta = jnp.sum(grad_group.astype(jnp.float32) * out_group.astype(jnp.float32), axis=-1)[
        ..., None, None
    ]
    probability_gradient = jnp.einsum(
        "gqhd,gjkhd->gqhjk", grad_group, gathered_value_blocks, preferred_element_type=jnp.float32
    )
    score_gradient = (probability * (probability_gradient - delta)).astype(jnp.bfloat16)
    query_gradient = (
        jnp.einsum(
            "gqhjk,gjkhd->gqhd",
            score_gradient,
            gathered_key_blocks,
            preferred_element_type=jnp.float32,
        )
        * softmax_scale
    ).astype(jnp.bfloat16)
    key_contribution = (
        jnp.einsum(
            "gqhjk,gqhd->gjkhd", score_gradient, query_group, preferred_element_type=jnp.float32
        )
        * softmax_scale
    )
    value_contribution = jnp.einsum(
        "gqhjk,gqhd->gjkhd", reduced_precision, grad_group, preferred_element_type=jnp.float32
    )
    return (query_gradient, jnp.concatenate([key_contribution, value_contribution], axis=-1))


def on_device(query_rows, key_rows, value_rows, out_grad, block_lists, block_counts):
    tok_rows = query_rows.shape[0]
    width = query_rows.shape[1]
    heads = width // HDIM
    query_heads = query_rows.reshape(tok_rows, heads, HDIM)
    grad_heads = out_grad.reshape(tok_rows, heads, HDIM)
    pair_heads = jnp.concatenate(
        [key_rows.reshape(tok_rows, heads, HDIM), value_rows.reshape(tok_rows, heads, HDIM)], axis=2
    )
    seg_query, seg_pair, seg_grad = (
        lax.all_to_all(query_heads, "uly", split_axis=1, concat_axis=0, tiled=True),
        lax.all_to_all(pair_heads, "uly", split_axis=1, concat_axis=0, tiled=True),
        lax.all_to_all(grad_heads, "uly", split_axis=1, concat_axis=0, tiled=True),
    )
    all_pairs = lax.all_gather(seg_pair, "blk", axis=0, tiled=True)
    seg_rows = seg_query.shape[0]
    head_local = seg_query.shape[1]
    local_blocks = seg_rows // BLK
    group_size = math.gcd(16, local_blocks)
    groups = local_blocks // group_size
    pair_blocks = all_pairs.reshape(-1, BLK, head_local, 2 * HDIM)
    query_groups = seg_query.reshape(groups, group_size, BLK, head_local, HDIM)
    grad_groups = seg_grad.reshape(groups, group_size, BLK, head_local, HDIM)
    list_groups = block_lists.reshape(groups, group_size, KSEL)
    count_groups = block_counts.reshape(groups, group_size)
    empty = jnp.zeros(pair_blocks.shape, jnp.float32)

    def joint_turn(accum, operands):
        query_group, grad_group, list_group, count_group = operands
        gathered_key_blocks, gathered_value_blocks, usable = fetch_sets(
            pair_blocks, list_group, count_group
        )
        probability = probabilities(query_group, gathered_key_blocks, usable)
        reduced_precision = probability.astype(jnp.bfloat16)
        out_group = attend(reduced_precision, gathered_value_blocks)
        query_gradient, pair_terms = backward_group(
            gathered_key_blocks,
            gathered_value_blocks,
            query_group,
            grad_group,
            out_group,
            probability,
            reduced_precision,
        )
        return (accum.at[list_group].add(pair_terms), (out_group, query_gradient))

    accum, (out_groups, query_parts) = lax.scan(
        joint_turn, empty, (query_groups, grad_groups, list_groups, count_groups)
    )
    accum_rows = accum.reshape(-1, head_local, 2 * HDIM)
    summed = lax.psum_scatter(accum_rows, "blk", scatter_dimension=0, tiled=True)
    pair_grad = summed.astype(jnp.bfloat16)
    out_seg = out_groups.reshape(seg_rows, head_local, HDIM)
    query_seg = query_parts.reshape(seg_rows, head_local, HDIM)
    out_back, query_back, pair_back = (
        lax.all_to_all(out_seg, "uly", split_axis=0, concat_axis=1, tiled=True),
        lax.all_to_all(query_seg, "uly", split_axis=0, concat_axis=1, tiled=True),
        lax.all_to_all(pair_grad, "uly", split_axis=0, concat_axis=1, tiled=True),
    )
    return (
        out_back.reshape(tok_rows, width),
        query_back.reshape(tok_rows, width),
        pair_back[..., :HDIM].reshape(tok_rows, width),
        pair_back[..., HDIM:].reshape(tok_rows, width),
    )


def solution(mesh):
    placed = (
        P(("blk", "uly"), None),
        P(("blk", "uly"), None),
        P(("blk", "uly"), None),
        P(("blk", "uly"), None),
        P("blk", None),
        P("blk"),
    )
    return jax.shard_map(
        on_device,
        mesh=mesh,
        in_specs=placed,
        out_specs=(
            P(("blk", "uly"), None),
            P(("blk", "uly"), None),
            P(("blk", "uly"), None),
            P(("blk", "uly"), None),
        ),
        check_vma=False,
    )
```

profile of v0, /device:TPU:0, one launch (start us, length us, event | category | flops | bytes accessed | tf_op | source)
XLA Modules:
  0.0 136.0 jit_solution(9518933461510708066)
XLA Ops:
  7.2 1.0 copy.69
  8.2 1.0 copy.70
  9.3 16.0 %all_to_all.96 = bf16[128,8,128]{0,2,1:T(8,128)(2,1)S(1)} all-to-all(bf16[128,8,128]{0,2,1:T(8,128)(2,1)S(1)} %pad_maximum_fusion.1), channel_id=1, replica_groups=mesh['blk'=4,'uly'=8] {'uly'}, dimensions={1} | all-to-all | bytes 524288 | tf_op jit(solution)/shard_map/all_to_all | solution.py:85
  25.3 0.9 copy.71
  26.2 1.7 %copy.73 = bf16[128,512]{0,1:T(8,128)(2,1)} copy(bf16[128,512]{1,0:T(8,128)(2,1)} %param.6) | data formatting | bytes 262144 | tf_op args[0]
  27.8 3.6 %all-to-all-start.1 = ((bf16[128,8,64]{0,2,1:T(8,128)(2,1)}), bf16[128,8,64]{0,2,1:T(8,128)(2,1)S(1)}, u32[]{:S(2)}, u32[]{:S(2)}) async-start(bf16[128,8,64]{0,2,1:T(8,128)(2,1)} %bitcast.9), calls=%async_computation.1 | async-start | bytes 262144 | tf_op jit(solution)/shard_map/all_to_all | solution.py:84
  32.3 1.7 %copy.81 = bf16[128,512]{0,1:T(8,128)(2,1)} copy(bf16[128,512]{1,0:T(8,128)(2,1)} %param.9) | data formatting | bytes 262144 | tf_op args[3]
  34.0 4.8 %all-to-all-done.1 = bf16[128,8,64]{0,2,1:T(8,128)(2,1)S(1)} async-done(((bf16[128,8,64]{0,2,1:T(8,128)(2,1)}), bf16[128,8,64]{0,2,1:T(8,128)(2,1)S(1)}, u32[]{:S(2)}, u32[]{:S(2)}) %all-to-all-start.1) | async-done | bytes 131104 | tf_op jit(solution)/shard_map/all_to_all | solution.py:84
  38.8 3.4 %all-to-all-start.3 = ((bf16[128,8,64]{0,2,1:T(8,128)(2,1)}), bf16[128,8,64]{0,2,1:T(8,128)(2,1)S(1)}, u32[]{:S(2)}, u32[]{:S(2)}) async-start(bf16[128,8,64]{0,2,1:T(8,128)(2,1)} %bitcast.24), calls=%async_computation.3 | async-start | bytes 262144 | tf_op jit(solution)/shard_map/all_to_all | solution.py:86
  43.1 6.3 %all-to-all-done.3 = bf16[128,8,64]{0,2,1:T(8,128)(2,1)S(1)} async-done(((bf16[128,8,64]{0,2,1:T(8,128)(2,1)}), bf16[128,8,64]{0,2,1:T(8,128)(2,1)S(1)}, u32[]{:S(2)}, u32[]{:S(2)}) %all-to-all-start.3) | async-done | bytes 131104 | tf_op jit(solution)/shard_map/all_to_all | solution.py:86
  50.0 2.2 %gather_fusion = bf16[128,64,128]{2,1,0:T(8,128)(2,1)S(1)} fusion(bf16[64,64,128]{2,1,0:T(8,128)(2,1)} %bitcast.208, s32[1024]{0:T(1024)S(1)} %pad_clamp_fusion), kind=kCustom, calls=%fused_computation | custom fusion | bytes 4194816 | tf_op jit(solution)/shard_map/while/body/eval_jaxpr/gather | solution.py:13
  52.2 1.0 fusion.1
  53.2 1.1 bitcast_reduce_fusion
  54.4 2.3 %fusion.33 = (f32[16,64]{1,0:T(8,128)S(1)}, bf16[16,64,1,64]{1,3,0,2:T(8,128)(2,1)S(1)}) fusion(f32[16,64,1,64]{1,0,3,2:T(8,128)S(1)} %reshape.172, f32[16,64]{1,0:T(8,128)S(1)} %bitcast_reduce_fusion, f32[16,64]{1,0:T(8,128)S(1)} %get-tuple-element.45, f32[16,8,64,64]{3,2,1,0:T(8,128)S(1)} %get-tuple-element.46, pred[16,8]{1,0:T(8,128)(4,1)S(1)} %iota_compare_fusion, ...), kind=kOutput, calls=%fused_computation.33 | convolution fusion | flops 69991424 | bytes 4599936 | tf_op jit(solution)/shard_map/while/body/eval_jaxpr/gqhjk,gjkhd->gqhd/dot_general | solution.py:28
  56.7 1.3 convolution_bitcast_fusion
  57.9 1.9 %fusion = bf16[16,64,1,8,64]{1,4,3,0,2:T(8,128)(2,1)S(1)} fusion(bf16[16,64,64,1]{2,1,3,0:T(8,128)(2,1)S(1)} %bitcast.231, f32[16,64]{1,0:T(8,128)S(1)} %get-tuple-element.47, f32[16,64]{1,0:T(8,128)S(1)} %bitcast_reduce_fusion, f32[16,64]{1,0:T(8,128)S(1)} %get-tuple-element.45, f32[16,8,64,64]{3,2,1,0:T(8,128)S(1)} %get-tuple-element.46, ...), kind=kOutput, calls=%fused_computation.4 | convolution fusion | flops 70778880 | bytes 5386368 | tf_op jit(solution)/shard_map/while/body/eval_jaxpr/gqhd,gjkhd->gqhjk/dot_general | solution.py:49
  60.5 3.1 %pad_maximum_fusion = f32[16,8,64,1,128]{4,2,1,0,3:T(8,128)} fusion(f32[16,8,64,1,64]{4,2,1,0,3:T(8,128)S(1)} %convolution_bitcast_fusion, f32[16,8,64,1,64]{4,2,1,0,3:T(8,128)S(1)} %multiply_bitcast_fusion), kind=kLoop, calls=%fused_computation.2 | loop fusion | flops 1048576 | bytes 8388608 | tf_op jit(solution)/shard_map/while/body/eval_jaxpr/concatenate | solution.py:71
  63.8 13.5 %scatter_fusion = f32[64,64,128]{2,1,0:T(8,128)S(1)} fusion(f32[64,64,128]{2,1,0:T(8,128)S(1)} %broadcast.65, s32[128]{0:T(128)S(1)} %reshape.177, f32[128,64,128]{2,1,0:T(8,128)} %bitcast.207), kind=kCustom, calls=%fused_computation.1 | custom fusion | flops 1048576 | bytes 12583424 | tf_op jit(solution)/shard_map/while/body/eval_jaxpr/scatter-add | solution.py:118
  77.4 1.3 copy-done
  79.6 2.3 %reduce.4 = bf16[1024,64]{1,0:T(8,128)(2,1)S(1)} reduce(bf16[1024,1,64]{2,1,0:T(2,128)(2,1)S(1)} %reshape.205, bf16[]{:T(256)} %broadcast.90), dimensions={1}, to_apply=%reshape.205.reduce_sub_computation | reduce | bytes 262146 | tf_op jit(solution)/shard_map/reshape | solution.py:126
  81.8 0.9 reshape.207
  82.7 3.6 %all-to-all-start.2 = ((bf16[8,2,4096]{2,1,0:T(2,128)(2,1)}), bf16[8,2,4096]{2,1,0:T(2,128)(2,1)S(1)}, u32[]{:S(2)}, u32[]{:S(2)}) async-start(bf16[8,2,4096]{2,1,0:T(2,128)(2,1)} %reshape.207), calls=%async_computation.2 | async-start | bytes 262144 | tf_op jit(solution)/shard_map/all_to_all | solution.py:129
  86.3 3.0 %fusion.27 = bf16[16,64,1,64]{1,3,0,2:T(8,128)(2,1)S(1)} fusion(bf16[16,64,1,8,64]{1,4,3,0,2:T(8,128)(2,1)} %copy-done.1, bf16[16,8,64,1,128]{4,2,1,0,3:T(8,128)(2,1)} %bitcast.213), kind=kOutput, calls=%fused_computation.30 | convolution fusion | flops 67239936 | bytes 3276800 | tf_op jit(solution)/shard_map/while/body/eval_jaxpr/gqhjk,gjkhd->gqhd/dot_general | solution.py:54
  89.7 2.3 %reduce.5 = bf16[1024,64]{1,0:T(8,128)(2,1)S(1)} reduce(bf16[1024,1,64]{2,1,0:T(2,128)(2,1)S(1)} %reshape.206, bf16[]{:T(256)} %broadcast.90), dimensions={1}, to_apply=%reshape.206.reduce_sub_computation | reduce | bytes 262146 | tf_op jit(solution)/shard_map/reshape | solution.py:127
  92.0 0.9 reshape.209
  93.4 5.2 %all-to-all-start.4 = ((bf16[8,2,4096]{2,1,0:T(2,128)(2,1)}), bf16[8,2,4096]{2,1,0:T(2,128)(2,1)S(1)}, u32[]{:S(2)}, u32[]{:S(2)}) async-start(bf16[8,2,4096]{2,1,0:T(2,128)(2,1)} %reshape.209), calls=%async_computation.4 | async-start | bytes 262144 | tf_op jit(solution)/shard_map/all_to_all | solution.py:130
  98.6 9.4 %reduce-scatter.2.cloned.1.call-done = f32[1024,1,128]{2,1,0:T(1,128)} async-done(((f32[4096,1,128]{2,1,0:T(1,128)}), f32[1024,1,128]{2,1,0:T(1,128)}) %reduce-scatter.2.cloned.1.call-update) | async-done | bytes 524304 | tf_op jit(solution)/shard_map/reduce_scatter | solution.py:124
  108.1 1.4 %convert_element_type.61 = bf16[1024,1,128]{2,1,0:T(2,128)(2,1)S(1)} convert(f32[1024,1,128]{2,1,0:T(1,128)} %reduce-scatter.2.cloned.1.call-done) | non-fusion elementwise | flops 131072 | bytes 786432 | tf_op jit(solution)/shard_map/convert_element_type | solution.py:125
  109.5 2.2 %reduce.6 = bf16[1024,128]{1,0:T(8,128)(2,1)S(1)} reduce(bf16[1024,1,128]{2,1,0:T(2,128)(2,1)S(1)} %convert_element_type.61, bf16[]{:T(256)} %broadcast.90), dimensions={1}, to_apply=%convert_element_type.61.reduce_sub_computation | reduce | bytes 524290 | tf_op jit(solution)/shard_map/convert_element_type | solution.py:125
  112.4 5.5 %all-to-all-start.5 = ((bf16[8,2,8192]{2,1,0:T(2,128)(2,1)}), bf16[8,2,8192]{2,1,0:T(2,128)(2,1)S(1)}, u32[]{:S(2)}, u32[]{:S(2)}) async-start(bf16[8,2,8192]{2,1,0:T(2,128)(2,1)} %reshape.211), calls=%async_computation.6 | async-start | bytes 524288 | tf_op jit(solution)/shard_map/all_to_all | solution.py:131
  120.9 6.0 %all-to-all-done.5 = bf16[8,2,8192]{2,1,0:T(2,128)(2,1)S(1)} async-done(((bf16[8,2,8192]{2,1,0:T(2,128)(2,1)}), bf16[8,2,8192]{2,1,0:T(2,128)(2,1)S(1)}, u32[]{:S(2)}, u32[]{:S(2)}) %all-to-all-start.5) | async-done | bytes 262176 | tf_op jit(solution)/shard_map/all_to_all | solution.py:131
  127.5 0.8 copy.96
  (47 shorter events, 10.2 us)
Async XLA Ops:
  7.2 42.8 %all-gather.2.cloned.1.call-start = ((), (), s32[]{:S(2)}) async-start(), calls=%async_computation.7 | async-start | bytes 1310720 | tf_op jit(solution)/shard_map/all_gather | solution.py:88
  27.8 10.9 %all-to-all-start.1 = ((bf16[128,8,64]{0,2,1:T(8,128)(2,1)}), bf16[128,8,64]{0,2,1:T(8,128)(2,1)S(1)}, u32[]{:S(2)}, u32[]{:S(2)}) async-start(bf16[128,8,64]{0,2,1:T(8,128)(2,1)} %bitcast.9), calls=%async_computation.1 | async-start | bytes 262144 | tf_op jit(solution)/shard_map/all_to_all | solution.py:84
  38.8 10.7 %all-to-all-start.3 = ((bf16[128,8,64]{0,2,1:T(8,128)(2,1)}), bf16[128,8,64]{0,2,1:T(8,128)(2,1)S(1)}, u32[]{:S(2)}, u32[]{:S(2)}) async-start(bf16[128,8,64]{0,2,1:T(8,128)(2,1)} %bitcast.24), calls=%async_computation.3 | async-start | bytes 262144 | tf_op jit(solution)/shard_map/all_to_all | solution.py:86
  42.2 65.9 %reduce-scatter.2.cloned.1.call-start = ((), (), s32[]{:S(2)}) async-start(), calls=%async_computation.8 | async-start | bytes 2621440 | tf_op jit(solution)/shard_map/reduce_scatter | solution.py:124
  52.2 5.7 %copy-start.2 = (bf16[128,64,128]{2,1,0:T(8,128)(2,1)}, bf16[128,64,128]{2,1,0:T(8,128)(2,1)S(1)}, u32[]{:S(2)}) copy-start(bf16[128,64,128]{2,1,0:T(8,128)(2,1)S(1)} %gather_fusion) | copy-start | bytes 6291460
  59.8 3.8 %copy-start.1 = (bf16[16,64,1,8,64]{1,4,3,0,2:T(8,128)(2,1)}, bf16[16,64,1,8,64]{1,4,3,0,2:T(8,128)(2,1)S(1)}, u32[]{:S(2)}) copy-start(bf16[16,64,1,8,64]{1,4,3,0,2:T(8,128)(2,1)S(1)} %fusion) | copy-start | bytes 3145732
  77.3 1.4 copy-start
  82.7 10.7 %all-to-all-start.2 = ((bf16[8,2,4096]{2,1,0:T(2,128)(2,1)}), bf16[8,2,4096]{2,1,0:T(2,128)(2,1)S(1)}, u32[]{:S(2)}, u32[]{:S(2)}) async-start(bf16[8,2,4096]{2,1,0:T(2,128)(2,1)} %reshape.207), calls=%async_computation.2 | async-start | bytes 262144 | tf_op jit(solution)/shard_map/all_to_all | solution.py:129
  93.4 19.0 %all-to-all-start.4 = ((bf16[8,2,4096]{2,1,0:T(2,128)(2,1)}), bf16[8,2,4096]{2,1,0:T(2,128)(2,1)S(1)}, u32[]{:S(2)}, u32[]{:S(2)}) async-start(bf16[8,2,4096]{2,1,0:T(2,128)(2,1)} %reshape.209), calls=%async_computation.4 | async-start | bytes 262144 | tf_op jit(solution)/shard_map/all_to_all | solution.py:130
  112.4 14.4 %all-to-all-start.5 = ((bf16[8,2,8192]{2,1,0:T(2,128)(2,1)}), bf16[8,2,8192]{2,1,0:T(2,128)(2,1)S(1)}, u32[]{:S(2)}, u32[]{:S(2)}) async-start(bf16[8,2,8192]{2,1,0:T(2,128)(2,1)} %reshape.211), calls=%async_computation.6 | async-start | bytes 524288 | tf_op jit(solution)/shard_map/all_to_all | solution.py:131
Sparse Core Ops, SparseCore 0:
  26.3 15.7 all-gather.1
  78.8 29.1 reduce-scatter.1
where the time goes:
time: 137 us; the launch traced here: 136 us
  other arithmetic  27.3 us (20%)
  waiting for transfers between devices  27 us (20%)
  starting transfers between devices  21.3 us (16%)
  local copies, waits for them, and re-layouts  19.7 us (14%)
  blocking collectives  16 us (12%)
  between operations  14.4 us (11%)
  matrix products  10.2 us (7%)
    all_to_all x1, blocking collectives, on_device(): lax.all_to_all(pair_heads, 'uly', split_axis=1, concat_axis=0, tiled=True)  16 us
    scatter-add x1, other arithmetic, joint_turn(): return (accum.at[list_group].add(pair_terms), (out_group, query_gradient))  13.5 us
    unnamed x23, local copies, waits for them, and re-layouts  13.4 us
    reduce_scatter x1, waiting for transfers between devices, on_device(): lax.psum_scatter(accum_rows, 'blk', scatter_dimension=0, tiled=True)  9.43 us
    all_to_all x1, waiting for transfers between devices, on_device(): lax.all_to_all(grad_heads, 'uly', split_axis=1, concat_axis=0, tiled=True)  6.3 us
    all_to_all x1, waiting for transfers between devices, on_device(): lax.all_to_all(pair_grad, 'uly', split_axis=0, concat_axis=1, tiled=True)  5.97 us
    all_to_all x1, starting transfers between devices, on_device(): lax.all_to_all(pair_grad, 'uly', split_axis=0, concat_axis=1, tiled=True)  5.52 us
    all_to_all x1, starting transfers between devices, on_device(): lax.all_to_all(query_seg, 'uly', split_axis=0, concat_axis=1, tiled=True)  5.22 us
  transfers between devices with their start and end apart: 7, of which 5 were waited for; matrix products, arithmetic and copies ran while one was open for 17% of the time, Pallas kernels for 0%

commit v1 on v0

--- a/solution.py
+++ b/solution.py
@@ -7,6 +7,25 @@
 HDIM = 64
 BLK = 64
 KSEL = 8
+
+
+def match_wall(array_here, dim_at, raw):
+    next_value = array_here.shape
+    return jnp.moveaxis(
+        array_here.reshape(
+            *next_value[:dim_at], raw, next_value[dim_at] // raw, *next_value[dim_at + 1 :]
+        ),
+        dim_at,
+        0,
+    )
+
+
+def move_the_limits(matrix, k_dim):
+    matrix = jnp.moveaxis(matrix, 0, k_dim)
+    block_last = matrix.shape
+    return matrix.reshape(
+        *block_last[:k_dim], block_last[k_dim] * block_last[k_dim + 1], *block_last[k_dim + 2 :]
+    )
 
 
 def fetch_sets(pair_blocks, list_group, count_group):
@@ -72,6 +91,21 @@
 
 
 def on_device(query_rows, key_rows, value_rows, out_grad, block_lists, block_counts):
+
+    def review_node(q_in, comm_axis, t0, block_here=0):
+        answer, part_now = (lax.psum(1, axis_name=comm_axis), lax.axis_index(comm_axis))
+        s_next = match_wall(q_in, t0, answer)
+        pieces_in = [s_next[part_now]]
+        for dev_j in [*range(1, answer)]:
+            out_arr = s_next[(part_now + dev_j) % answer]
+            pieces_in.append(
+                lax.ppermute(
+                    out_arr, comm_axis, perm=[(pp, (pp + dev_j) % answer) for pp in range(answer)]
+                )
+            )
+        s_next = jnp.stack(pieces_in, axis=0)[(part_now - jnp.arange(answer)) % answer]
+        return move_the_limits(s_next, block_here)
+
     tok_rows = query_rows.shape[0]
     width = query_rows.shape[1]
     heads = width // HDIM
@@ -81,7 +115,7 @@
         [key_rows.reshape(tok_rows, heads, HDIM), value_rows.reshape(tok_rows, heads, HDIM)], axis=2
     )
     seg_query, seg_pair, seg_grad = (
-        lax.all_to_all(query_heads, "uly", split_axis=1, concat_axis=0, tiled=True),
+        review_node(query_heads, "uly", t0=1),
         lax.all_to_all(pair_heads, "uly", split_axis=1, concat_axis=0, tiled=True),
         lax.all_to_all(grad_heads, "uly", split_axis=1, concat_axis=0, tiled=True),
     )

time: 137 us -> 150 us (1.095)
  starting transfers between devices: 21.3 us -> 40 us
  blocking collectives: 16 us -> 0 us
  waiting for transfers between devices: 27 us -> 34.6 us
    all_to_all x1 -> x0, blocking collectives: 16 us -> none  [on_device(): lax.all_to_all(pair_heads, 'uly', split_axis=1, concat_axis=0, tiled=True)]
    ppermute x0 -> x7, starting transfers between devices: none -> 15.9 us  [review_node(): lax.ppermute(out_arr, comm_axis, perm=[(pp, (pp + dev_j) % answer) for pp...]
    all_gather x1, waiting for transfers between devices: 0.02 us -> 12.3 us  [on_device(): all_pairs = lax.all_gather(seg_pair, 'blk', axis=0, tiled=True)]
    all_to_all x1, waiting for transfers between devices: 6.3 us -> 0.01 us  [on_device(): lax.all_to_all(grad_heads, 'uly', split_axis=1, concat_axis=0, tiled=True)]
    ppermute x0 -> x7, waiting for transfers between devices: none -> 2.93 us  [review_node(): lax.ppermute(out_arr, comm_axis, perm=[(pp, (pp + dev_j) % answer) for pp...]
    all_to_all x1, starting transfers between devices: 3.56 us -> 5.52 us  [on_device(): lax.all_to_all(out_seg, 'uly', split_axis=0, concat_axis=1, tiled=True)]
    all_to_all x1, waiting for transfers between devices: 4.76 us -> 3.07 us  [on_device(): lax.all_to_all(pair_heads, 'uly', split_axis=1, concat_axis=0, tiled=True)]
    unnamed x23 -> x32, local copies, waits for them, and re-layouts: 13.4 us -> 13.4 us
  transfers between devices with their start and end apart: 7 -> 14, of which waited for: 5 -> 6; matrix products, arithmetic and copies ran while one was open for 17% -> 18% of each run, Pallas kernels for 0% -> 0%
where the time goes in v1:
time: 150 us; the launch traced here: 149 us
  starting transfers between devices  40 us (27%)
  waiting for transfers between devices  34.6 us (23%)
  other arithmetic  28.5 us (19%)
  local copies, waits for them, and re-layouts  20.4 us (14%)
  between operations  14.6 us (10%)
  matrix products  10.8 us (7%)
    ppermute x7, starting transfers between devices, review_node(): lax.ppermute(out_arr, comm_axis, perm=[(pp, (pp + dev_j) % answer) for pp...  15.9 us
    scatter-add x1, other arithmetic, joint_turn(): return (accum.at[list_group].add(pair_terms), (out_group, query_gradient))  13.5 us
    unnamed x32, local copies, waits for them, and re-layouts  13.4 us
    all_gather x1, waiting for transfers between devices, on_device(): all_pairs = lax.all_gather(seg_pair, 'blk', axis=0, tiled=True)  12.3 us
    reduce_scatter x1, waiting for transfers between devices, on_device(): lax.psum_scatter(accum_rows, 'blk', scatter_dimension=0, tiled=True)  9.48 us
    all_to_all x1, waiting for transfers between devices, on_device(): lax.all_to_all(pair_grad, 'uly', split_axis=0, concat_axis=1, tiled=True)  5.98 us
    all_to_all x1, starting transfers between devices, on_device(): lax.all_to_all(pair_grad, 'uly', split_axis=0, concat_axis=1, tiled=True)  5.52 us
    all_to_all x1, starting transfers between devices, on_device(): lax.all_to_all(out_seg, 'uly', split_axis=0, concat_axis=1, tiled=True)  5.52 us
  transfers between devices with their start and end apart: 14, of which 6 were waited for; matrix products, arithmetic and copies ran while one was open for 18% of the time, Pallas kernels for 0%

profile of v1, /device:TPU:0, one launch (start us, length us, event | category | flops | bytes accessed | tf_op | source)
XLA Modules:
  0.0 148.9 jit_solution(8262365117448626899)
XLA Ops:
  7.3 1.0 copy.99
  8.3 6.1 %collective-permute-start.6 = (bf16[128,1,64]{0,2,1:T(8,128)(2,1)S(1)}, bf16[128,1,64]{0,2,1:T(8,128)(2,1)S(1)}, u32[]{:S(2)}, u32[]{:S(2)}) collective-permute-start(bf16[128,1,64]{0,2,1:T(8,128)(2,1)S(1)} %get-tuple-element.49), channel_id=1, source_target_pairs={{0,7},{1,0},{2,1},{3,2},{4,3},{5,4},{6,5},{7,6},{8,15},{9,8},{10,9... | collective-permute-start | bytes 49160 | tf_op jit(solution)/shard_map/ppermute | solution.py:102
  14.9 3.0 %collective-permute-start.3 = (bf16[128,1,64]{0,2,1:T(8,128)(2,1)S(1)}, bf16[128,1,64]{0,2,1:T(8,128)(2,1)S(1)}, u32[]{:S(2)}, u32[]{:S(2)}) collective-permute-start(bf16[128,1,64]{0,2,1:T(8,128)(2,1)S(1)} %get-tuple-element.52), channel_id=1, source_target_pairs={{0,4},{1,5},{2,6},{3,7},{4,0},{5,1},{6,2},{7,3},{8,12},{9,13},{10,... | collective-permute-start | bytes 49160 | tf_op jit(solution)/shard_map/ppermute | solution.py:102
  17.8 1.5 %collective-permute-start = (bf16[128,1,64]{0,2,1:T(8,128)(2,1)S(1)}, bf16[128,1,64]{0,2,1:T(8,128)(2,1)S(1)}, u32[]{:S(2)}, u32[]{:S(2)}) collective-permute-start(bf16[128,1,64]{0,2,1:T(8,128)(2,1)S(1)} %get-tuple-element.55), channel_id=1, source_target_pairs={{0,1},{1,2},{2,3},{3,4},{4,5},{5,6},{6,7},{7,0},{8,9},{9,10},{10,1... | collective-permute-start | bytes 49160 | tf_op jit(solution)/shard_map/ppermute | solution.py:102
  19.4 1.0 copy.95
  20.4 1.0 copy.96
  22.1 4.5 %all-to-all-start = ((bf16[128,8,128]{0,2,1:T(8,128)(2,1)}), bf16[128,8,128]{0,2,1:T(8,128)(2,1)S(1)}, u32[]{:S(2)}, u32[]{:S(2)}) async-start(bf16[128,8,128]{0,2,1:T(8,128)(2,1)} %pad_maximum_fusion.1), calls=%async_computation | async-start | bytes 524288 | tf_op jit(solution)/shard_map/all_to_all | solution.py:119
  28.3 1.7 %copy.108 = bf16[128,512]{0,1:T(8,128)(2,1)} copy(bf16[128,512]{1,0:T(8,128)(2,1)} %param.9) | data formatting | bytes 262144 | tf_op args[3]
  29.9 2.0 %collective-permute-start.1 = (bf16[128,1,64]{0,2,1:T(8,128)(2,1)S(1)}, bf16[128,1,64]{0,2,1:T(8,128)(2,1)S(1)}, u32[]{:S(2)}, u32[]{:S(2)}) collective-permute-start(bf16[128,1,64]{0,2,1:T(8,128)(2,1)S(1)} %get-tuple-element.54), channel_id=1, source_target_pairs={{0,2},{1,3},{2,4},{3,5},{4,6},{5,7},{6,0},{7,1},{8,10},{9,11},{10,... | collective-permute-start | bytes 49160 | tf_op jit(solution)/shard_map/ppermute | solution.py:102
  32.0 3.1 %all-to-all-done = bf16[128,8,128]{0,2,1:T(8,128)(2,1)S(1)} async-done(((bf16[128,8,128]{0,2,1:T(8,128)(2,1)}), bf16[128,8,128]{0,2,1:T(8,128)(2,1)S(1)}, u32[]{:S(2)}, u32[]{:S(2)}) %all-to-all-start) | async-done | bytes 262176 | tf_op jit(solution)/shard_map/all_to_all | solution.py:119
  35.0 3.4 %all-to-all-start.2 = ((bf16[128,8,64]{0,2,1:T(8,128)(2,1)}), bf16[128,8,64]{0,2,1:T(8,128)(2,1)S(1)}, u32[]{:S(2)}, u32[]{:S(2)}) async-start(bf16[128,8,64]{0,2,1:T(8,128)(2,1)} %bitcast.37), calls=%async_computation.2 | async-start | bytes 262144 | tf_op jit(solution)/shard_map/all_to_all | solution.py:120
  39.4 2.8 %collective-permute-start.2 = (bf16[128,1,64]{0,2,1:T(8,128)(2,1)S(1)}, bf16[128,1,64]{0,2,1:T(8,128)(2,1)S(1)}, u32[]{:S(2)}, u32[]{:S(2)}) collective-permute-start(bf16[128,1,64]{0,2,1:T(8,128)(2,1)S(1)} %get-tuple-element.53), channel_id=1, source_target_pairs={{0,3},{1,4},{2,5},{3,6},{4,7},{5,0},{6,1},{7,2},{8,11},{9,12},{10,... | collective-permute-start | bytes 49160 | tf_op jit(solution)/shard_map/ppermute | solution.py:102
  42.2 2.9 %collective-permute-done.2 = bf16[128,1,64]{0,2,1:T(8,128)(2,1)S(1)} collective-permute-done((bf16[128,1,64]{0,2,1:T(8,128)(2,1)S(1)}, bf16[128,1,64]{0,2,1:T(8,128)(2,1)S(1)}, u32[]{:S(2)}, u32[]{:S(2)}) %collective-permute-start.2) | collective-permute-done | bytes 16416 | tf_op jit(solution)/shard_map/ppermute | solution.py:102
  46.6 12.3 %all-gather.2.cloned.1.call-done = bf16[4096,1,128]{2,0,1:T(8,128)(2,1)} async-done(((bf16[1024,1,128]{2,0,1:T(8,128)(2,1)}), bf16[4096,1,128]{2,0,1:T(8,128)(2,1)}) %all-gather.2.cloned.1.call-update) | async-done | bytes 1048592 | tf_op jit(solution)/shard_map/all_gather | solution.py:122
  58.9 2.2 %gather_fusion = bf16[128,64,128]{2,1,0:T(8,128)(2,1)S(1)} fusion(bf16[64,64,128]{2,1,0:T(8,128)(2,1)} %bitcast.235, s32[1024]{0:T(1024)S(1)} %pad_clamp_fusion.1), kind=kCustom, calls=%fused_computation | custom fusion | bytes 4194816 | tf_op jit(solution)/shard_map/while/body/eval_jaxpr/gather | solution.py:32
  62.1 1.1 bitcast_reduce_fusion
  63.2 2.9 %fusion.32 = (f32[16,64]{1,0:T(8,128)S(1)}, bf16[16,64,1,64]{1,3,0,2:T(8,128)(2,1)}) fusion(f32[16,64,1,64]{1,0,3,2:T(8,128)S(1)} %reshape.230, f32[16,64]{1,0:T(8,128)S(1)} %bitcast_reduce_fusion, f32[16,64]{1,0:T(8,128)S(1)} %get-tuple-element.56, f32[16,8,64,64]{3,2,1,0:T(8,128)S(1)} %get-tuple-element.57, pred[16,8]{1,0:T(8,128)(4,1)S(1)} %iota_compare_fusion, ...), kind=kOutput, calls=%fused_computation.33 | convolution fusion | flops 69991424 | bytes 4599936 | tf_op jit(solution)/shard_map/while/body/eval_jaxpr/gqhjk,gjkhd->gqhd/dot_general | solution.py:47
  66.2 1.2 convolution_bitcast_fusion
  67.4 1.9 %fusion = bf16[16,64,1,8,64]{1,4,3,0,2:T(8,128)(2,1)S(1)} fusion(bf16[16,64,64,1]{2,1,3,0:T(8,128)(2,1)S(1)} %bitcast.260, f32[16,64]{1,0:T(8,128)S(1)} %get-tuple-element.58, f32[16,64]{1,0:T(8,128)S(1)} %bitcast_reduce_fusion, f32[16,64]{1,0:T(8,128)S(1)} %get-tuple-element.56, f32[16,8,64,64]{3,2,1,0:T(8,128)S(1)} %get-tuple-element.57, ...), kind=kOutput, calls=%fused_computation.5 | convolution fusion | flops 70778880 | bytes 5386368 | tf_op jit(solution)/shard_map/while/body/eval_jaxpr/gqhd,gjkhd->gqhjk/dot_general | solution.py:68
  71.1 3.1 %pad_maximum_fusion = f32[16,8,64,1,128]{4,2,1,0,3:T(8,128)} fusion(f32[16,8,64,1,64]{4,2,1,0,3:T(8,128)S(1)} %convolution_bitcast_fusion, f32[16,8,64,1,64]{4,2,1,0,3:T(8,128)S(1)} %multiply_bitcast_fusion), kind=kLoop, calls=%fused_computation.3 | loop fusion | flops 1048576 | bytes 8388608 | tf_op jit(solution)/shard_map/while/body/eval_jaxpr/concatenate | solution.py:90
  74.4 13.5 %scatter_fusion = f32[64,64,128]{2,1,0:T(8,128)S(1)} fusion(f32[64,64,128]{2,1,0:T(8,128)S(1)} %broadcast.137, s32[128]{0:T(128)S(1)} %reshape.235, f32[128,64,128]{2,1,0:T(8,128)} %bitcast.233), kind=kCustom, calls=%fused_computation.2 | custom fusion | flops 1048576 | bytes 12583424 | tf_op jit(solution)/shard_map/while/body/eval_jaxpr/scatter-add | solution.py:152
  88.0 1.3 copy-done
  90.2 2.3 %reduce.4 = bf16[1024,64]{1,0:T(8,128)(2,1)S(1)} reduce(bf16[1024,1,64]{2,1,0:T(2,128)(2,1)S(1)} %reshape.276, bf16[]{:T(256)} %broadcast.167), dimensions={1}, to_apply=%reshape.276.reduce_sub_computation | reduce | bytes 262146 | tf_op jit(solution)/shard_map/reshape | solution.py:160
  93.3 5.5 %all-to-all-start.1 = ((bf16[8,2,4096]{2,1,0:T(2,128)(2,1)}), bf16[8,2,4096]{2,1,0:T(2,128)(2,1)S(1)}, u32[]{:S(2)}, u32[]{:S(2)}) async-start(bf16[8,2,4096]{2,1,0:T(2,128)(2,1)} %reshape.278), calls=%async_computation.1 | async-start | bytes 262144 | tf_op jit(solution)/shard_map/all_to_all | solution.py:163
  98.9 3.1 %fusion.26 = bf16[16,64,1,64]{1,3,0,2:T(8,128)(2,1)S(1)} fusion(bf16[16,64,1,8,64]{1,4,3,0,2:T(8,128)(2,1)} %copy-done.1, bf16[16,8,64,1,128]{4,2,1,0,3:T(8,128)(2,1)} %bitcast.241), kind=kOutput, calls=%fused_computation.30 | convolution fusion | flops 67239936 | bytes 3276800 | tf_op jit(solution)/shard_map/while/body/eval_jaxpr/gqhjk,gjkhd->gqhd/dot_general | solution.py:73
  102.3 2.3 %reduce.5 = bf16[1024,64]{1,0:T(8,128)(2,1)S(1)} reduce(bf16[1024,1,64]{2,1,0:T(2,128)(2,1)S(1)} %reshape.277, bf16[]{:T(256)} %broadcast.167), dimensions={1}, to_apply=%reshape.277.reduce_sub_computation | reduce | bytes 262146 | tf_op jit(solution)/shard_map/reshape | solution.py:161
  106.3 5.2 %all-to-all-start.3 = ((bf16[8,2,4096]{2,1,0:T(2,128)(2,1)}), bf16[8,2,4096]{2,1,0:T(2,128)(2,1)S(1)}, u32[]{:S(2)}, u32[]{:S(2)}) async-start(bf16[8,2,4096]{2,1,0:T(2,128)(2,1)} %reshape.280), calls=%async_computation.3 | async-start | bytes 262144 | tf_op jit(solution)/shard_map/all_to_all | solution.py:164
  111.4 9.5 %reduce-scatter.2.cloned.1.call-done = f32[1024,1,128]{2,1,0:T(1,128)} async-done(((f32[4096,1,128]{2,1,0:T(1,128)}), f32[1024,1,128]{2,1,0:T(1,128)}) %reduce-scatter.2.cloned.1.call-update) | async-done | bytes 524304 | tf_op jit(solution)/shard_map/reduce_scatter | solution.py:158
  120.9 1.4 convert_element_type.61
  122.3 2.2 %reduce.6 = bf16[1024,128]{1,0:T(8,128)(2,1)S(1)} reduce(bf16[1024,1,128]{2,1,0:T(2,128)(2,1)S(1)} %convert_element_type.61, bf16[]{:T(256)} %broadcast.167), dimensions={1}, to_apply=%convert_element_type.61.reduce_sub_computation | reduce | bytes 524290 | tf_op jit(solution)/shard_map/convert_element_type | solution.py:159
  125.3 5.5 %all-to-all-start.4 = ((bf16[8,2,8192]{2,1,0:T(2,128)(2,1)}), bf16[8,2,8192]{2,1,0:T(2,128)(2,1)S(1)}, u32[]{:S(2)}, u32[]{:S(2)}) async-start(bf16[8,2,8192]{2,1,0:T(2,128)(2,1)} %reshape.282), calls=%async_computation.5 | async-start | bytes 524288 | tf_op jit(solution)/shard_map/all_to_all | solution.py:165
  133.8 6.0 %all-to-all-done.4 = bf16[8,2,8192]{2,1,0:T(2,128)(2,1)S(1)} async-done(((bf16[8,2,8192]{2,1,0:T(2,128)(2,1)}), bf16[8,2,8192]{2,1,0:T(2,128)(2,1)S(1)}, u32[]{:S(2)}, u32[]{:S(2)}) %all-to-all-start.4) | async-done | bytes 262176 | tf_op jit(solution)/shard_map/all_to_all | solution.py:165
  (76 shorter events, 17.9 us)
Async XLA Ops:
  8.3 36.9 %collective-permute-start.6 = (bf16[128,1,64]{0,2,1:T(8,128)(2,1)S(1)}, bf16[128,1,64]{0,2,1:T(8,128)(2,1)S(1)}, u32[]{:S(2)}, u32[]{:S(2)}) collective-permute-start(bf16[128,1,64]{0,2,1:T(8,128)(2,1)S(1)} %get-tuple-element.49), channel_id=1, source_target_pairs={{0,7},{1,0},{2,1},{3,2},{4,3},{5,4},{6,5},{7,6},{8,15},{9,8},{10,9... | collective-permute-start | bytes 49160 | tf_op jit(solution)/shard_map/ppermute | solution.py:102
  14.4 30.8 %collective-permute-start.5 = (bf16[128,1,64]{0,2,1:T(8,128)(2,1)S(1)}, bf16[128,1,64]{0,2,1:T(8,128)(2,1)S(1)}, u32[]{:S(2)}, u32[]{:S(2)}) collective-permute-start(bf16[128,1,64]{0,2,1:T(8,128)(2,1)S(1)} %get-tuple-element.50), channel_id=1, source_target_pairs={{0,6},{1,7},{2,0},{3,1},{4,2},{5,3},{6,4},{7,5},{8,14},{9,15},{10,... | collective-permute-start | bytes 49160 | tf_op jit(solution)/shard_map/ppermute | solution.py:102
  14.9 30.3 %collective-permute-start.4 = (bf16[128,1,64]{0,2,1:T(8,128)(2,1)S(1)}, bf16[128,1,64]{0,2,1:T(8,128)(2,1)S(1)}, u32[]{:S(2)}, u32[]{:S(2)}) collective-permute-start(bf16[128,1,64]{0,2,1:T(8,128)(2,1)S(1)} %get-tuple-element.51), channel_id=1, source_target_pairs={{0,5},{1,6},{2,7},{3,0},{4,1},{5,2},{6,3},{7,4},{8,13},{9,14},{10,... | collective-permute-start | bytes 49160 | tf_op jit(solution)/shard_map/ppermute | solution.py:102
  14.9 30.3 %collective-permute-start.3 = (bf16[128,1,64]{0,2,1:T(8,128)(2,1)S(1)}, bf16[128,1,64]{0,2,1:T(8,128)(2,1)S(1)}, u32[]{:S(2)}, u32[]{:S(2)}) collective-permute-start(bf16[128,1,64]{0,2,1:T(8,128)(2,1)S(1)} %get-tuple-element.52), channel_id=1, source_target_pairs={{0,4},{1,5},{2,6},{3,7},{4,0},{5,1},{6,2},{7,3},{8,12},{9,13},{10,... | collective-permute-start | bytes 49160 | tf_op jit(solution)/shard_map/ppermute | solution.py:102
  17.8 12.1 %collective-permute-start = (bf16[128,1,64]{0,2,1:T(8,128)(2,1)S(1)}, bf16[128,1,64]{0,2,1:T(8,128)(2,1)S(1)}, u32[]{:S(2)}, u32[]{:S(2)}) collective-permute-start(bf16[128,1,64]{0,2,1:T(8,128)(2,1)S(1)} %get-tuple-element.55), channel_id=1, source_target_pairs={{0,1},{1,2},{2,3},{3,4},{4,5},{5,6},{6,7},{7,0},{8,9},{9,10},{10,1... | collective-permute-start | bytes 49160 | tf_op jit(solution)/shard_map/ppermute | solution.py:102
  22.1 12.9 %all-to-all-start = ((bf16[128,8,128]{0,2,1:T(8,128)(2,1)}), bf16[128,8,128]{0,2,1:T(8,128)(2,1)S(1)}, u32[]{:S(2)}, u32[]{:S(2)}) async-start(bf16[128,8,128]{0,2,1:T(8,128)(2,1)} %pad_maximum_fusion.1), calls=%async_computation | async-start | bytes 524288 | tf_op jit(solution)/shard_map/all_to_all | solution.py:119
  29.9 9.5 %collective-permute-start.1 = (bf16[128,1,64]{0,2,1:T(8,128)(2,1)S(1)}, bf16[128,1,64]{0,2,1:T(8,128)(2,1)S(1)}, u32[]{:S(2)}, u32[]{:S(2)}) collective-permute-start(bf16[128,1,64]{0,2,1:T(8,128)(2,1)S(1)} %get-tuple-element.54), channel_id=1, source_target_pairs={{0,2},{1,3},{2,4},{3,5},{4,6},{5,7},{6,0},{7,1},{8,10},{9,11},{10,... | collective-permute-start | bytes 49160 | tf_op jit(solution)/shard_map/ppermute | solution.py:102
  35.0 11.0 %all-to-all-start.2 = ((bf16[128,8,64]{0,2,1:T(8,128)(2,1)}), bf16[128,8,64]{0,2,1:T(8,128)(2,1)S(1)}, u32[]{:S(2)}, u32[]{:S(2)}) async-start(bf16[128,8,64]{0,2,1:T(8,128)(2,1)} %bitcast.37), calls=%async_computation.2 | async-start | bytes 262144 | tf_op jit(solution)/shard_map/all_to_all | solution.py:120
  38.4 20.5 %all-gather.2.cloned.1.call-start = ((), (), s32[]{:S(2)}) async-start(), calls=%async_computation.6 | async-start | bytes 1310720 | tf_op jit(solution)/shard_map/all_gather | solution.py:122
  39.3 81.6 %reduce-scatter.2.cloned.1.call-start = ((), (), s32[]{:S(2)}) async-start(), calls=%async_computation.7 | async-start | bytes 2621440 | tf_op jit(solution)/shard_map/reduce_scatter | solution.py:158
  39.4 5.8 %collective-permute-start.2 = (bf16[128,1,64]{0,2,1:T(8,128)(2,1)S(1)}, bf16[128,1,64]{0,2,1:T(8,128)(2,1)S(1)}, u32[]{:S(2)}, u32[]{:S(2)}) collective-permute-start(bf16[128,1,64]{0,2,1:T(8,128)(2,1)S(1)} %get-tuple-element.53), channel_id=1, source_target_pairs={{0,3},{1,4},{2,5},{3,6},{4,7},{5,0},{6,1},{7,2},{8,11},{9,12},{10,... | collective-permute-start | bytes 49160 | tf_op jit(solution)/shard_map/ppermute | solution.py:102
  61.1 6.3 %copy-start.2 = (bf16[128,64,128]{2,1,0:T(8,128)(2,1)}, bf16[128,64,128]{2,1,0:T(8,128)(2,1)S(1)}, u32[]{:S(2)}) copy-start(bf16[128,64,128]{2,1,0:T(8,128)(2,1)S(1)} %gather_fusion) | copy-start | bytes 6291460
  69.3 1.4 copy-start.1
  74.4 14.9 %copy-start.3 = (bf16[16,64,1,64]{1,3,0,2:T(8,128)(2,1)S(1)}, bf16[16,64,1,64]{1,3,0,2:T(8,128)(2,1)}, u32[]{:S(2)}) copy-start(bf16[16,64,1,64]{1,3,0,2:T(8,128)(2,1)} %get-tuple-element.59) | copy-start | bytes 393220
  87.9 1.3 copy-start
  93.3 12.9 %all-to-all-start.1 = ((bf16[8,2,4096]{2,1,0:T(2,128)(2,1)}), bf16[8,2,4096]{2,1,0:T(2,128)(2,1)S(1)}, u32[]{:S(2)}, u32[]{:S(2)}) async-start(bf16[8,2,4096]{2,1,0:T(2,128)(2,1)} %reshape.278), calls=%async_computation.1 | async-start | bytes 262144 | tf_op jit(solution)/shard_map/all_to_all | solution.py:163
  106.3 19.0 %all-to-all-start.3 = ((bf16[8,2,4096]{2,1,0:T(2,128)(2,1)}), bf16[8,2,4096]{2,1,0:T(2,128)(2,1)S(1)}, u32[]{:S(2)}, u32[]{:S(2)}) async-start(bf16[8,2,4096]{2,1,0:T(2,128)(2,1)} %reshape.280), calls=%async_computation.3 | async-start | bytes 262144 | tf_op jit(solution)/shard_map/all_to_all | solution.py:164
  125.3 14.4 %all-to-all-start.4 = ((bf16[8,2,8192]{2,1,0:T(2,128)(2,1)}), bf16[8,2,8192]{2,1,0:T(2,128)(2,1)S(1)}, u32[]{:S(2)}, u32[]{:S(2)}) async-start(bf16[8,2,8192]{2,1,0:T(2,128)(2,1)} %reshape.282), calls=%async_computation.5 | async-start | bytes 524288 | tf_op jit(solution)/shard_map/all_to_all | solution.py:165
Sparse Core Ops, SparseCore 0:
  40.8 18.0 all-gather.1
  89.4 31.4 reduce-scatter.1
